TPU v7x, 32 devices: a whole 2x2x4 slice. The times are simulated.
32 devices in a mesh: energy: 16 (over z, x, core), mom: 2 (over y).
Axes of the slice: x: 2, y: 2, z: 4, core: 2. Of those that a mesh axis runs over, the one named last changes fastest.
Arguments:
- sigma_in: float32 [64, 2, 2, 256, 256], P('energy', 'mom'), may hold values from -0.1875 to 0.1875
- hamiltonian: float32 [2, 2, 256, 256], P('mom'), may hold values from -0.375 to 0.375
- coupling: float32 [2, 256, 256], P('mom'), may hold values from -0.1875 to 0.1875
- energies: float32 [64], replicated, may hold values from 1.4 to 2, as said below
- counts: int32 [64], replicated, may hold values from 2 to 4, as said below
- strengths: float32 [16], replicated, may hold values from 0.05625 to 0.1875
- offsets: int32 [16], replicated, may hold values from 0 to 1
Outputs:
- sigma_next: float32 [64, 2, 2, 256, 256], P('energy', 'mom')
Inputs may be any that keep to these rules, and one draw needn't show every extreme that they name: `energies`: increasing along the grid. `counts`: each point needs either 2 or 4 sweeps, and some point needs 4.
All inputs are finite; a program needn't handle non-finite values.
Results may differ from a plain program's by a relative error of at most 0.0003.
Values sent between devices are 32-bit elements; how exact they have to be, the bound alone decides.
A program may use at most 64 MiB of HBM per device.

v0:
```python
import functools

import jax
import jax.numpy as jnp
from jax import lax
from jax.experimental import pallas as pl
from jax.experimental.pallas import tpu as pltpu
from jax.sharding import PartitionSpec as P

PRECISE = lax.Precision.HIGHEST
MIX_RATE = 0.6
PHONON = 0.1
BROADENING = 0.02


def shifted(value, axis, steps):
    count = lax.axis_size(axis)
    pairs = [(source, (source + steps) % count) for source in range(count)]
    return lax.ppermute(value, axis, pairs)


def product(left_side, right_side):
    return jnp.dot(left_side, right_side, precision=PRECISE, preferred_element_type=jnp.float32)


def invert(matrix, energy, sweeps):
    identity = jnp.eye(matrix.shape[0], dtype=jnp.float32)

    def keep_going(carried):
        return carried[0] < sweeps

    def sweep(carried):
        estimate = carried[1]
        return (carried[0] + 1, 2.0 * estimate - product(estimate, product(matrix, estimate)))

    return lax.while_loop(keep_going, sweep, (jnp.int32(0), identity / energy))[1]


def solve_point(ham_block, coupling_block, sigma_pair, energy, sweeps):
    identity = jnp.eye(ham_block.shape[1], dtype=jnp.float32)
    left_matrix = energy * identity - ham_block[0] - sigma_pair[0]
    left_inverse = invert(left_matrix, energy, sweeps)
    inverse_coupled = product(left_inverse, coupling_block)
    coupled_inverse = product(coupling_block.T, left_inverse)
    right_matrix = (
        energy * identity
        - ham_block[1]
        - sigma_pair[1]
        - product(coupling_block.T, inverse_coupled)
    )
    right_green = invert(right_matrix, energy, sweeps)
    left_green = left_inverse + product(product(inverse_coupled, right_green), coupled_inverse)
    return jnp.stack([left_green, right_green])


def lorentz(offset):
    scaled = offset / BROADENING
    return 1.0 / (1.0 + scaled * scaled)


def build_kernel(row_energy, column_energy):
    spacing = row_energy[:, None] - column_energy[None, :]
    kernel = lorentz(spacing - PHONON) + lorentz(spacing + PHONON)
    return kernel / jnp.sum(kernel, axis=1, keepdims=True)


def plain_body(sigma_in, hamiltonian, coupling, energies, counts, strengths, offsets):
    points = sigma_in.shape[0]
    order = sigma_in.shape[3]
    ranks = lax.axis_size("energy")
    moments = lax.axis_size("mom")
    my_rank = lax.axis_index("energy")
    own_energy = lax.dynamic_slice_in_dim(energies, my_rank * points, points)
    own_count = lax.dynamic_slice_in_dim(counts, my_rank * points, points)
    blocks = sigma_in[:, 0]

    def solve_held(held_point):
        return solve_point(hamiltonian[0], coupling[0], held_point[0], held_point[1], held_point[2])

    green_blocks = lax.map(solve_held, (blocks, own_energy, own_count))
    shift_index = jnp.arange(moments, dtype=jnp.int32)
    weights = jnp.sum(
        strengths[:, None] * (offsets[:, None] == shift_index[None, :]).astype(jnp.float32), axis=0
    )
    kernel = build_kernel(energies, energies)
    piece_width = 2 * order * order // ranks
    spread = green_blocks.reshape(points, ranks, moments, piece_width // moments)
    column = lax.all_to_all(spread, "energy", split_axis=1, concat_axis=0, tiled=True)[:, 0]
    rows_all = column.shape[0]
    flat_column = column.reshape(rows_all, -1)
    mixed_sum = weights[0] * flat_column
    for offset_step in range(1, moments):
        mixed_sum = mixed_sum + weights[offset_step] * shifted(flat_column, "mom", offset_step)
    sigma_part = product(kernel, mixed_sum).reshape(column.shape)
    result = lax.all_to_all(sigma_part[:, None], "energy", split_axis=0, concat_axis=1, tiled=True)
    sigma_new = result.reshape(sigma_in.shape)
    return (1.0 - MIX_RATE) * sigma_in + MIX_RATE * sigma_new


SUBLANES = 8
TOGETHER = 1
MESH_ID = pl.DeviceIdType.MESH


def split(value):
    high = value.astype(jnp.bfloat16)
    return high, (value - high.astype(jnp.float32)).astype(jnp.bfloat16)


def left_parts(value):
    high, low = split(value)
    return jnp.concatenate([high, low, high], axis=1)


def right_parts(value):
    high, low = split(value)
    return jnp.concatenate([high, high, low], axis=0)


def multiply(left_side, right_side):
    return jnp.dot(left_side, right_side, preferred_element_type=jnp.float32)


def series(ratios, energies, counts, identity):
    order = identity.shape[0]
    squares = [multiply(left_parts(r), right_parts(r)) for r in ratios]
    totals = [identity + r for r in ratios]
    for sweep in (1, 2, 3):
        rights = [right_parts(s) for s in squares]
        if sweep < 3:
            both = [
                multiply(jnp.concatenate([left_parts(t), left_parts(s)], axis=0), q)
                for t, s, q in zip(totals, squares, rights)
            ]
            added = [b[:order] for b in both]
            squares = [b[order:] for b in both]
        else:
            added = [multiply(left_parts(t), q) for t, q in zip(totals, rights)]
        totals = [jnp.where(sweep < c, t + a, t) for t, a, c in zip(totals, added, counts)]
    return [t * (1.0 / e) for t, e in zip(totals, energies)]


def kernel(
    ranks, moments, points, order, held,
    energy_ref, count_ref, strength_ref, offset_ref, sigma_hbm, ham_ref, coupling_ref,
    out_ref,
    green, gathered, mixed_out, wide, across, across_t,
    sigma_ref, read_sem, send_first, recv_first, send_second, recv_second,
):
    devices = ranks * moments
    total = ranks * points
    my_rank = lax.axis_index("energy")
    my_moment = lax.axis_index("mom")
    me = my_rank * moments + my_moment
    reads = [
        pltpu.make_async_copy(sigma_hbm.at[point], sigma_ref.at[point], read_sem.at[point])
        for point in range(points)
    ]
    for read in reads:
        read.start()
    barrier = pltpu.get_barrier_semaphore()

    def greet(index, carried):
        other = lax.rem(me + index, devices)
        pl.semaphore_signal(
            barrier, inc=1,
            device_id={"energy": other // moments, "mom": lax.rem(other, moments)},
            device_id_type=MESH_ID,
        )
        return carried

    lax.fori_loop(1, devices, greet, 0)

    across[...] = right_parts(coupling_ref[...])
    across_t[...] = left_parts(coupling_ref[...].T)
    row_index = lax.broadcasted_iota(jnp.int32, (order, order), 0)
    identity = (row_index == lax.broadcasted_iota(jnp.int32, (order, order), 1)).astype(jnp.float32)

    def place_of(other):
        return {"energy": other // moments, "mom": lax.rem(other, moments)}

    def give_first(source, landing, piece):
        pltpu.make_async_copy(source(me), landing, recv_first.at[piece]).start()

        def give(index, carried):
            other = lax.rem(me + index, devices)
            pltpu.make_async_remote_copy(
                src_ref=source(other),
                dst_ref=landing,
                send_sem=send_first,
                recv_sem=recv_first.at[piece],
                device_id=place_of(other),
                device_id_type=MESH_ID,
            ).start()
            return carried

        lax.fori_loop(1, devices, give, 0)

    def solve(group, carried):
        chosen = [group * TOGETHER + index for index in range(TOGETHER)]
        for point in chosen:
            pltpu.make_async_copy(sigma_hbm.at[point], sigma_ref.at[point], read_sem.at[point]).wait()
        energies = [energy_ref[my_rank * points + point] for point in chosen]
        counts = [count_ref[my_rank * points + point] for point in chosen]
        ratios = [(ham_ref[0] + sigma_ref[point, 0]) * (1.0 / e) for point, e in zip(chosen, energies)]
        left_inverses = series(ratios, energies, counts, identity)
        coupled = [multiply(left_parts(x), across[...]) for x in left_inverses]
        backs = [multiply(across_t[...], right_parts(x)) for x in left_inverses]
        folds = [multiply(across_t[...], right_parts(x)) for x in coupled]
        ratios = [
            (ham_ref[1] + sigma_ref[point, 1] + fold) * (1.0 / e)
            for point, e, fold in zip(chosen, energies, folds)
        ]
        right_greens = series(ratios, energies, counts, identity)
        inner = [multiply(left_parts(c), right_parts(x)) for c, x in zip(coupled, right_greens)]
        left_greens = [
            x + multiply(left_parts(i), right_parts(b)) for x, i, b in zip(left_inverses, inner, backs)
        ]
        tiles = order // SUBLANES
        for point, left_green, right_green in zip(chosen, left_greens, right_greens):
            green[point, :tiles] = left_green.reshape(tiles, SUBLANES, order)
            green[point, tiles:] = right_green.reshape(tiles, SUBLANES, order)

        @pl.when(group == 0)
        def _():
            pl.semaphore_wait(barrier, devices - 1)

        for point in chosen:
            landing = gathered.at[my_moment, 0, my_rank * points + point]
            give_first(lambda other: green.at[point, other * held], landing, 0)
        return carried

    lax.fori_loop(0, points // TOGETHER, solve, 0)

    for piece in range(1, held):
        landing = gathered.at[my_moment, piece, pl.ds(my_rank * points, points)]
        give_first(lambda other: green.at[:, other * held + piece], landing, piece)

    span = total * SUBLANES
    column = lax.broadcasted_iota(jnp.int32, (SUBLANES, span), 1)
    lane_slot = lax.rem(column, SUBLANES)
    lane_point = lax.div(column, SUBLANES)
    same = lane_slot == lax.broadcasted_iota(jnp.int32, (SUBLANES, span), 0)

    def place(index, carried):
        return jnp.where(lane_point == index, energy_ref[index], carried)

    column_energy = lax.fori_loop(0, total, place, jnp.zeros((SUBLANES, span), jnp.float32))

    def build(index, carried):
        spacing = energy_ref[index] - column_energy
        row = lorentz(spacing - PHONON) + lorentz(spacing + PHONON)
        row = jnp.where(same, row, 0.0)
        row = row * (MIX_RATE / jnp.sum(row, axis=1, keepdims=True))
        wide[pl.ds(pl.multiple_of(index * SUBLANES, SUBLANES), SUBLANES), :] = row
        return carried

    lax.fori_loop(0, total, build, 0)
    weights = []
    for step in range(moments):
        weight = jnp.float32(0.0)
        for transfer in range(strength_ref.shape[0]):
            weight = weight + jnp.where(offset_ref[transfer] == step, strength_ref[transfer], 0.0)
        weights.append(weight)

    wide_parts = left_parts(wide[...])
    for piece in range(held):
        arrived = gathered.at[:, piece]
        pltpu.make_async_copy(arrived, arrived, recv_first.at[piece]).wait()
        for turn in range(moments):
            moment = lax.rem(my_moment + 1 + turn, moments)
            scattered = weights[0] * gathered[moment, piece]
            for step in range(1, moments):
                source = lax.rem(moment - step + moments, moments)
                scattered = scattered + weights[step] * gathered[source, piece]
            result = multiply(wide_parts, right_parts(scattered.reshape(span, order)))
            mixed_out[moment, piece] = result.reshape(total, SUBLANES, order)

            def give_back(index, carried, moment=moment, piece=piece):
                rank = lax.rem(my_rank + index, ranks)
                pltpu.make_async_remote_copy(
                    src_ref=mixed_out.at[moment, piece, pl.ds(rank * points, points)],
                    dst_ref=out_ref.at[:, me * held + piece],
                    send_sem=send_second,
                    recv_sem=recv_second,
                    device_id={"energy": rank, "mom": moment},
                    device_id_type=MESH_ID,
                ).start()
                return carried

            if turn < moments - 1:
                lax.fori_loop(0, ranks, give_back, 0)
            else:
                lax.fori_loop(1, ranks, give_back, 0)
                pltpu.make_async_copy(
                    mixed_out.at[my_moment, piece, pl.ds(my_rank * points, points)],
                    out_ref.at[:, me * held + piece],
                    recv_second,
                ).start()

    pltpu.make_async_copy(out_ref, out_ref, recv_second).wait()
    sent = green.at[:, pl.ds(0, (devices - 1) * held)]
    pltpu.make_async_copy(sent, sent, send_first).wait()
    pltpu.make_async_copy(sent, sent, send_second).wait()


def fused_body(sigma_in, hamiltonian, coupling, energies, counts, strengths, offsets):
    points, order = sigma_in.shape[0], sigma_in.shape[3]
    ranks = lax.axis_size("energy")
    moments = lax.axis_size("mom")
    tiles = 2 * order // SUBLANES
    held = tiles // (ranks * moments)
    span = ranks * points * SUBLANES
    smem = pl.BlockSpec(memory_space=pltpu.SMEM)
    vmem = pl.BlockSpec(memory_space=pltpu.VMEM)
    sigma_new = pl.pallas_call(
        functools.partial(kernel, ranks, moments, points, order, held),
        out_shape=jax.ShapeDtypeStruct((points, tiles, SUBLANES, order), jnp.float32),
        in_specs=[smem] * 4 + [pl.BlockSpec(memory_space=pl.ANY)] + [vmem] * 2,
        out_specs=pl.BlockSpec(memory_space=pl.ANY),
        scratch_shapes=[
            pltpu.VMEM((points, tiles, SUBLANES, order), jnp.float32),
            pltpu.VMEM((moments, held, ranks * points, SUBLANES, order), jnp.float32),
            pltpu.VMEM((moments, held, ranks * points, SUBLANES, order), jnp.float32),
            pltpu.VMEM((span, span), jnp.float32),
            pltpu.VMEM((3 * order, order), jnp.bfloat16),
            pltpu.VMEM((order, 3 * order), jnp.bfloat16),
            pltpu.VMEM((points, 2, order, order), jnp.float32),
            pltpu.SemaphoreType.DMA((points,)),
            pltpu.SemaphoreType.DMA,
            pltpu.SemaphoreType.DMA((held,)),
            pltpu.SemaphoreType.DMA,
            pltpu.SemaphoreType.DMA,
        ],
        compiler_params=pltpu.CompilerParams(
            collective_id=0, has_side_effects=True, vmem_limit_bytes=60 * 1024 * 1024
        ),
        name="green_and_scatter",
    )(energies, counts, strengths, offsets, sigma_in[:, 0], hamiltonian[0], coupling[0])
    return (1.0 - MIX_RATE) * sigma_in + sigma_new.reshape(sigma_in.shape)


def body(sigma_in, hamiltonian, coupling, energies, counts, strengths, offsets):
    devices = lax.axis_size("energy") * lax.axis_size("mom")
    tiles = 2 * sigma_in.shape[3] // SUBLANES
    fits = tiles % devices == 0 and devices % 2 == 0 and sigma_in.shape[0] % TOGETHER == 0
    chosen = fused_body if fits else plain_body
    return chosen(sigma_in, hamiltonian, coupling, energies, counts, strengths, offsets)


def solution(mesh):
    placed = (
        P("energy", "mom", None, None, None),
        P("mom", None, None, None),
        P("mom", None, None),
        P(),
        P(),
        P(),
        P(),
    )
    return jax.shard_map(
        body,
        mesh=mesh,
        in_specs=placed,
        out_specs=P("energy", "mom", None, None, None),
        check_vma=False,
    )
```

profile of v0, /device:TPU:8, one launch (start us, length us, event | category | flops | bytes accessed | tf_op | source)
XLA Modules:
  0.0 102.0 jit_solution(8195465045457201603)
XLA Ops:
  0.0 0.0 copy-start
  0.0 98.7 %green_and_scatter.1 = f32[4,64,8,256]{3,2,1,0:T(8,128)} custom-call(f32[64]{0:T(128)} %energy_ref.1, s32[64]{0:T(128)} %count_ref.1, f32[16]{0:T(128)} %strength_ref.1, s32[16]{0:T(128)} %offset_ref.1, f32[4,2,256,256]{3,2,1,0:T(8,128)} %bitcast.6, f32[2,256,256]{2,1,0:T(8,128)} %bitcast.8, f32[256,256]{1,0:T(8,128)} %bitcast.9), custom_call_target="tpu_custom_call" | custom-call | tf_op jit(solution)/shard_map/green_and_scatter/pallas_call | solution.py:316
  98.8 0.0 copy-done
  98.8 3.2 %multiply_add_fusion = f32[4,1,2,256,256]{4,3,2,1,0:T(8,128)} fusion(f32[4,1,2,256,256]{4,3,2,1,0:T(8,128)} %bitcast.7, f32[4,1,2,256,256]{4,3,2,1,0:T(8,128)S(1)} %copy-done), kind=kLoop, calls=%fused_computation | loop fusion | flops 1048576 | bytes 6291456 | tf_op jit(solution)/shard_map/add | solution.py:340
Async XLA Ops:
  0.0 98.8 %copy-start = (f32[4,1,2,256,256]{4,3,2,1,0:T(8,128)S(1)}, f32[4,1,2,256,256]{4,3,2,1,0:T(8,128)}, u32[]{:S(2)}) copy-start(f32[4,1,2,256,256]{4,3,2,1,0:T(8,128)} %param.7) | copy-start | bytes 6291460
where the time goes:
time: 103 us; the launch traced here: 102 us
  Pallas kernels  98.7 us (96%)
  other arithmetic  3.18 us (3%)
    pallas_call x1, Pallas kernels, fused_body(): pl.pallas_call(functools.partial(kernel, ranks, moments, points, order, h...  98.7 us
    add x1, other arithmetic, fused_body(): return (1.0 - MIX_RATE) * sigma_in + sigma_new.reshape(sigma_in.shape)  3.18 us

commit v1 on v0

--- a/solution.py
+++ b/solution.py
@@ -98,7 +98,6 @@
 
 
 SUBLANES = 8
-TOGETHER = 1
 MESH_ID = pl.DeviceIdType.MESH
 
 
@@ -142,100 +141,154 @@
 
 def kernel(
     ranks, moments, points, order, held,
-    energy_ref, count_ref, strength_ref, offset_ref, sigma_hbm, ham_ref, coupling_ref,
+    energy_hbm, count_hbm, strength_hbm, offset_hbm, sigma_hbm, ham_hbm, coupling_hbm,
     out_ref,
     green, gathered, mixed_out, wide, across, across_t,
-    sigma_ref, read_sem, send_first, recv_first, send_second, recv_second,
+    sigma_ref, ham_ref, coupling_ref, energy_ref, count_ref, strength_ref, offset_ref,
+    ready, read_sigma, read_other, send_first, recv_first, send_second, recv_second,
 ):
     devices = ranks * moments
+    side = devices // 2
+    group = side // 2
     total = ranks * points
+    early = held // 2
+    cuts = 2 if order % 256 == 0 else 1
+    width = order // cuts
     my_rank = lax.axis_index("energy")
     my_moment = lax.axis_index("mom")
     me = my_rank * moments + my_moment
-    reads = [
-        pltpu.make_async_copy(sigma_hbm.at[point], sigma_ref.at[point], read_sem.at[point])
+    my_side = me // side
+    spot = lax.rem(me, side)
+    near_side = my_side * side
+    far_side = (1 - my_side) * side
+
+    def place_of(other):
+        return {"energy": other // moments, "mom": lax.rem(other, moments)}
+
+    sources = [
+        (ham_hbm, ham_ref), (energy_hbm, energy_ref), (count_hbm, count_ref),
+        (coupling_hbm, coupling_ref), (strength_hbm, strength_ref), (offset_hbm, offset_ref),
+    ]
+    reads = [pltpu.make_async_copy(a, b, read_other.at[n]) for n, (a, b) in enumerate(sources)]
+    sigma_reads = [
+        pltpu.make_async_copy(sigma_hbm.at[point], sigma_ref.at[point], read_sigma.at[point])
         for point in range(points)
     ]
-    for read in reads:
+    for read in [reads[0], sigma_reads[0]] + reads[1:4]:
         read.start()
     barrier = pltpu.get_barrier_semaphore()
 
     def greet(index, carried):
-        other = lax.rem(me + index, devices)
-        pl.semaphore_signal(
-            barrier, inc=1,
-            device_id={"energy": other // moments, "mom": lax.rem(other, moments)},
-            device_id_type=MESH_ID,
-        )
+        other = far_side + lax.rem(spot + index, side)
+        pl.semaphore_signal(barrier, inc=1, device_id=place_of(other), device_id_type=MESH_ID)
         return carried
 
-    lax.fori_loop(1, devices, greet, 0)
-
-    across[...] = right_parts(coupling_ref[...])
-    across_t[...] = left_parts(coupling_ref[...].T)
+    lax.fori_loop(0, side, greet, 0)
+    for read in sigma_reads[1:] + reads[4:]:
+        read.start()
+
     row_index = lax.broadcasted_iota(jnp.int32, (order, order), 0)
     identity = (row_index == lax.broadcasted_iota(jnp.int32, (order, order), 1)).astype(jnp.float32)
 
-    def place_of(other):
-        return {"energy": other // moments, "mom": lax.rem(other, moments)}
-
-    def give_first(source, landing, piece):
-        pltpu.make_async_copy(source(me), landing, recv_first.at[piece]).start()
-
-        def give(index, carried):
-            other = lax.rem(me + index, devices)
+    def tile_of(other, piece):
+        return (held - 1 - piece) * devices + other
+
+    def send_over(send):
+        def over(index, carried):
+            turn = lax.div(index, group)
+            half = turn * (1 - my_side) + (1 - turn) * my_side
+            half = 1 - half
+            send(far_side + half * group + lax.rem(spot + index, group))
+            return carried
+
+        lax.fori_loop(0, side, over, 0)
+
+    def send_within(send):
+        def within(index, carried):
+            send(near_side + lax.rem(spot + index, side))
+            return carried
+
+        lax.fori_loop(1, side, within, 0)
+
+    def first_of(point, piece, cut):
+        semaphore = recv_first.at[piece if piece < early else early + (piece - early) * cuts + cut]
+        chosen = slice(None) if piece < early else pl.ds(cut * width, width)
+        if piece < early:
+            landing = gathered.at[my_moment, piece, my_rank * points + point]
+            source_of = lambda other: green.at[point, tile_of(other, piece)]
+        else:
+            landing = gathered.at[my_moment, piece, pl.ds(my_rank * points, points), :, chosen]
+            source_of = lambda other: green.at[:, tile_of(other, piece), :, chosen]
+
+        def send(other):
             pltpu.make_async_remote_copy(
-                src_ref=source(other),
-                dst_ref=landing,
-                send_sem=send_first,
-                recv_sem=recv_first.at[piece],
-                device_id=place_of(other),
-                device_id_type=MESH_ID,
+                src_ref=source_of(other), dst_ref=landing,
+                send_sem=send_first, recv_sem=semaphore,
+                device_id=place_of(other), device_id_type=MESH_ID,
             ).start()
-            return carried
-
-        lax.fori_loop(1, devices, give, 0)
-
-    def solve(group, carried):
-        chosen = [group * TOGETHER + index for index in range(TOGETHER)]
-        for point in chosen:
-            pltpu.make_async_copy(sigma_hbm.at[point], sigma_ref.at[point], read_sem.at[point]).wait()
-        energies = [energy_ref[my_rank * points + point] for point in chosen]
-        counts = [count_ref[my_rank * points + point] for point in chosen]
-        ratios = [(ham_ref[0] + sigma_ref[point, 0]) * (1.0 / e) for point, e in zip(chosen, energies)]
-        left_inverses = series(ratios, energies, counts, identity)
-        coupled = [multiply(left_parts(x), across[...]) for x in left_inverses]
-        backs = [multiply(across_t[...], right_parts(x)) for x in left_inverses]
-        folds = [multiply(across_t[...], right_parts(x)) for x in coupled]
-        ratios = [
-            (ham_ref[1] + sigma_ref[point, 1] + fold) * (1.0 / e)
-            for point, e, fold in zip(chosen, energies, folds)
-        ]
-        right_greens = series(ratios, energies, counts, identity)
-        inner = [multiply(left_parts(c), right_parts(x)) for c, x in zip(coupled, right_greens)]
-        left_greens = [
-            x + multiply(left_parts(i), right_parts(b)) for x, i, b in zip(left_inverses, inner, backs)
-        ]
-        tiles = order // SUBLANES
-        for point, left_green, right_green in zip(chosen, left_greens, right_greens):
-            green[point, :tiles] = left_green.reshape(tiles, SUBLANES, order)
-            green[point, tiles:] = right_green.reshape(tiles, SUBLANES, order)
-
-        @pl.when(group == 0)
+
+        def keep():
+            pltpu.make_async_copy(source_of(me), landing, semaphore).start()
+
+        return send, keep
+
+    for read in reads[:3]:
+        read.wait()
+    tiles = order // SUBLANES
+
+    def solve(point, carried):
+        pltpu.make_async_copy(sigma_hbm.at[point], sigma_ref.at[point], read_sigma.at[point]).wait()
+        energy = energy_ref[my_rank * points + point]
+        count = count_ref[my_rank * points + point]
+        ratio = (ham_ref[0] + sigma_ref[point, 0]) * (1.0 / energy)
+        left_inverse = series([ratio], [energy], [count], identity)[0]
+
+        @pl.when(point == 0)
         def _():
-            pl.semaphore_wait(barrier, devices - 1)
-
-        for point in chosen:
-            landing = gathered.at[my_moment, 0, my_rank * points + point]
-            give_first(lambda other: green.at[point, other * held], landing, 0)
+            reads[3].wait()
+            across[...] = right_parts(coupling_ref[...])
+            across_t[...] = left_parts(coupling_ref[...].T)
+
+        coupled = multiply(left_parts(left_inverse), across[...])
+        fold = multiply(across_t[...], right_parts(coupled))
+        ratio = (ham_ref[1] + sigma_ref[point, 1] + fold) * (1.0 / energy)
+        right_green = series([ratio], [energy], [count], identity)[0]
+        green[point, tiles:] = right_green.reshape(tiles, SUBLANES, order)
+
+        @pl.when(point == 0)
+        def _():
+            pl.semaphore_wait(barrier, side)
+            mirror = lax.rem(me + side, devices)
+            pl.semaphore_signal(ready, inc=1, device_id=place_of(mirror), device_id_type=MESH_ID)
+
+        for piece in range(early):
+            send_over(first_of(point, piece, 0)[0])
+        back = multiply(across_t[...], right_parts(left_inverse))
+        inner = multiply(left_parts(coupled), right_parts(right_green))
+        left_green = left_inverse + multiply(left_parts(inner), right_parts(back))
+        green[point, :tiles] = left_green.reshape(tiles, SUBLANES, order)
+
+        @pl.when(point == 0)
+        def _():
+            pl.semaphore_wait(ready, 1)
+
+        for piece in range(early):
+            send, keep = first_of(point, piece, 0)
+            keep()
+            send_within(send)
         return carried
 
-    lax.fori_loop(0, points // TOGETHER, solve, 0)
-
-    for piece in range(1, held):
-        landing = gathered.at[my_moment, piece, pl.ds(my_rank * points, points)]
-        give_first(lambda other: green.at[:, other * held + piece], landing, piece)
-
+    lax.fori_loop(0, points, solve, 0)
+
+    for piece in range(early, held):
+        for cut in range(cuts):
+            send, keep = first_of(0, piece, cut)
+            keep()
+            send_over(send)
+            send_within(send)
+
+    for read in reads[4:]:
+        read.wait()
     span = total * SUBLANES
     column = lax.broadcasted_iota(jnp.int32, (SUBLANES, span), 1)
     lane_slot = lax.rem(column, SUBLANES)
@@ -264,39 +317,40 @@
         weights.append(weight)
 
     wide_parts = left_parts(wide[...])
-    for piece in range(held):
-        arrived = gathered.at[:, piece]
-        pltpu.make_async_copy(arrived, arrived, recv_first.at[piece]).wait()
-        for turn in range(moments):
-            moment = lax.rem(my_moment + 1 + turn, moments)
-            scattered = weights[0] * gathered[moment, piece]
+    arrivals = [(piece, 0, slice(None)) for piece in range(early)] + [
+        (piece, cut, slice(cut * width, (cut + 1) * width))
+        for piece in range(early, held) for cut in range(cuts)
+    ]
+    for number, (piece, cut, chosen) in enumerate(arrivals):
+        arrived = gathered.at[:, piece, :, :, chosen]
+        pltpu.make_async_copy(arrived, arrived, recv_first.at[number]).wait()
+        for moment in range(moments):
+            scattered = weights[0] * gathered[moment, piece, :, :, chosen]
             for step in range(1, moments):
-                source = lax.rem(moment - step + moments, moments)
-                scattered = scattered + weights[step] * gathered[source, piece]
-            result = multiply(wide_parts, right_parts(scattered.reshape(span, order)))
-            mixed_out[moment, piece] = result.reshape(total, SUBLANES, order)
-
-            def give_back(index, carried, moment=moment, piece=piece):
-                rank = lax.rem(my_rank + index, ranks)
-                pltpu.make_async_remote_copy(
-                    src_ref=mixed_out.at[moment, piece, pl.ds(rank * points, points)],
-                    dst_ref=out_ref.at[:, me * held + piece],
-                    send_sem=send_second,
-                    recv_sem=recv_second,
-                    device_id={"energy": rank, "mom": moment},
-                    device_id_type=MESH_ID,
-                ).start()
-                return carried
-
-            if turn < moments - 1:
-                lax.fori_loop(0, ranks, give_back, 0)
-            else:
-                lax.fori_loop(1, ranks, give_back, 0)
-                pltpu.make_async_copy(
-                    mixed_out.at[my_moment, piece, pl.ds(my_rank * points, points)],
-                    out_ref.at[:, me * held + piece],
-                    recv_second,
-                ).start()
+                source = (moment - step) % moments
+                scattered = scattered + weights[step] * gathered[source, piece, :, :, chosen]
+            columns = scattered.shape[-1]
+            result = multiply(wide_parts, right_parts(scattered.reshape(span, columns)))
+            mixed_out[moment, piece, :, :, chosen] = result.reshape(total, SUBLANES, columns)
+
+        def give_back(other, piece=piece, chosen=chosen):
+            rank = other // moments
+            pltpu.make_async_remote_copy(
+                src_ref=mixed_out.at[lax.rem(other, moments), piece, pl.ds(rank * points, points), :, chosen],
+                dst_ref=out_ref.at[:, tile_of(me, piece), :, chosen],
+                send_sem=send_second,
+                recv_sem=recv_second,
+                device_id=place_of(other),
+                device_id_type=MESH_ID,
+            ).start()
+
+        send_within(give_back)
+        send_over(give_back)
+        pltpu.make_async_copy(
+            mixed_out.at[my_moment, piece, pl.ds(my_rank * points, points), :, chosen],
+            out_ref.at[:, tile_of(me, piece), :, chosen],
+            recv_second,
+        ).start()
 
     pltpu.make_async_copy(out_ref, out_ref, recv_second).wait()
     sent = green.at[:, pl.ds(0, (devices - 1) * held)]
@@ -310,40 +364,50 @@
     moments = lax.axis_size("mom")
     tiles = 2 * order // SUBLANES
     held = tiles // (ranks * moments)
-    span = ranks * points * SUBLANES
-    smem = pl.BlockSpec(memory_space=pltpu.SMEM)
-    vmem = pl.BlockSpec(memory_space=pltpu.VMEM)
+    total = ranks * points
+    span = total * SUBLANES
+    cuts = 2 if order % 256 == 0 else 1
+    hbm = pl.BlockSpec(memory_space=pltpu.HBM)
+    operands = (energies, counts, strengths, offsets, sigma_in[:, 0], hamiltonian[0], coupling[0])
     sigma_new = pl.pallas_call(
         functools.partial(kernel, ranks, moments, points, order, held),
         out_shape=jax.ShapeDtypeStruct((points, tiles, SUBLANES, order), jnp.float32),
-        in_specs=[smem] * 4 + [pl.BlockSpec(memory_space=pl.ANY)] + [vmem] * 2,
-        out_specs=pl.BlockSpec(memory_space=pl.ANY),
+        in_specs=[hbm] * 7,
+        out_specs=pl.BlockSpec(memory_space=pltpu.VMEM),
         scratch_shapes=[
             pltpu.VMEM((points, tiles, SUBLANES, order), jnp.float32),
-            pltpu.VMEM((moments, held, ranks * points, SUBLANES, order), jnp.float32),
-            pltpu.VMEM((moments, held, ranks * points, SUBLANES, order), jnp.float32),
+            pltpu.VMEM((moments, held, total, SUBLANES, order), jnp.float32),
+            pltpu.VMEM((moments, held, total, SUBLANES, order), jnp.float32),
             pltpu.VMEM((span, span), jnp.float32),
             pltpu.VMEM((3 * order, order), jnp.bfloat16),
             pltpu.VMEM((order, 3 * order), jnp.bfloat16),
             pltpu.VMEM((points, 2, order, order), jnp.float32),
+            pltpu.VMEM((2, order, order), jnp.float32),
+            pltpu.VMEM((order, order), jnp.float32),
+            pltpu.SMEM(energies.shape, jnp.float32),
+            pltpu.SMEM(counts.shape, jnp.int32),
+            pltpu.SMEM(strengths.shape, jnp.float32),
+            pltpu.SMEM(offsets.shape, jnp.int32),
+            pltpu.SemaphoreType.REGULAR,
             pltpu.SemaphoreType.DMA((points,)),
+            pltpu.SemaphoreType.DMA((6,)),
             pltpu.SemaphoreType.DMA,
-            pltpu.SemaphoreType.DMA((held,)),
+            pltpu.SemaphoreType.DMA((held // 2 * (1 + cuts),)),
             pltpu.SemaphoreType.DMA,
             pltpu.SemaphoreType.DMA,
         ],
         compiler_params=pltpu.CompilerParams(
-            collective_id=0, has_side_effects=True, vmem_limit_bytes=60 * 1024 * 1024
+            collective_id=0, has_side_effects=True, vmem_limit_bytes=32 * 1024 * 1024
         ),
         name="green_and_scatter",
-    )(energies, counts, strengths, offsets, sigma_in[:, 0], hamiltonian[0], coupling[0])
+    )(*[pltpu.with_memory_space_constraint(value, pltpu.HBM) for value in operands])
     return (1.0 - MIX_RATE) * sigma_in + sigma_new.reshape(sigma_in.shape)
 
 
 def body(sigma_in, hamiltonian, coupling, energies, counts, strengths, offsets):
     devices = lax.axis_size("energy") * lax.axis_size("mom")
     tiles = 2 * sigma_in.shape[3] // SUBLANES
-    fits = tiles % devices == 0 and devices % 2 == 0 and sigma_in.shape[0] % TOGETHER == 0
+    fits = tiles % (2 * devices) == 0 and lax.axis_size("energy") % 4 == 0
     chosen = fused_body if fits else plain_body
     return chosen(sigma_in, hamiltonian, coupling, energies, counts, strengths, offsets)
 

time: 103 us -> 101 us (0.981)
  other arithmetic: 3.18 us -> 1.59 us
    add x1, other arithmetic: 3.18 us -> 1.59 us  [fused_body(): return (1.0 - MIX_RATE) * sigma_in + sigma_new.reshape(sigma_in.shape)]
where the time goes in v1:
time: 101 us
  Pallas kernels  99 us (98%)
  other arithmetic  1.59 us (2%)
    pallas_call x1, Pallas kernels, fused_body(): pl.pallas_call(functools.partial(kernel, ranks, moments, points, order, h...  99 us

profile of v1, /device:TPU:8, one launch (start us, length us, event | category | flops | bytes accessed | tf_op | source)
XLA Modules:
  0.0 100.7 jit_solution(13246975479698027638)
XLA Ops:
  0.0 0.0 copy-start
  0.0 99.0 %green_and_scatter.1 = f32[4,64,8,256]{3,2,1,0:T(8,128)S(1)} custom-call(f32[64]{0:T(128)} %energy_hbm.1, s32[64]{0:T(128)} %count_hbm.1, f32[16]{0:T(128)} %strength_hbm.1, s32[16]{0:T(128)} %offset_hbm.1, f32[4,2,256,256]{3,2,1,0:T(8,128)} %bitcast.7, f32[2,256,256]{2,1,0:T(8,128)} %bitcast.8, f32[256,256]{1,0:T(8,128)} %bitcast.9), custom_call_target="tpu_custom_call" | custom-call | tf_op jit(solution)/shard_map/green_and_scatter/pallas_call | solution.py:372
  99.1 0.0 copy-done
  99.1 1.6 %multiply_add_fusion = f32[4,1,2,256,256]{4,3,2,1,0:T(8,128)} fusion(f32[4,1,2,256,256]{4,3,2,1,0:T(8,128)S(1)} %bitcast.6, f32[4,1,2,256,256]{4,3,2,1,0:T(8,128)S(1)} %copy-done), kind=kLoop, calls=%fused_computation | loop fusion | flops 1048576 | bytes 6291456 | tf_op jit(solution)/shard_map/add | solution.py:404
Async XLA Ops:
  0.0 99.1 %copy-start = (f32[4,1,2,256,256]{4,3,2,1,0:T(8,128)S(1)}, f32[4,1,2,256,256]{4,3,2,1,0:T(8,128)}, u32[]{:S(2)}) copy-start(f32[4,1,2,256,256]{4,3,2,1,0:T(8,128)} %param.7) | copy-start | bytes 6291460

commit v2 on v1

--- a/solution.py
+++ b/solution.py
@@ -120,31 +120,28 @@
     return jnp.dot(left_side, right_side, preferred_element_type=jnp.float32)
 
 
-def series(ratios, energies, counts, identity):
+def series(ratio, energy, count, identity):
     order = identity.shape[0]
-    squares = [multiply(left_parts(r), right_parts(r)) for r in ratios]
-    totals = [identity + r for r in ratios]
-    for sweep in (1, 2, 3):
-        rights = [right_parts(s) for s in squares]
-        if sweep < 3:
-            both = [
-                multiply(jnp.concatenate([left_parts(t), left_parts(s)], axis=0), q)
-                for t, s, q in zip(totals, squares, rights)
-            ]
-            added = [b[:order] for b in both]
-            squares = [b[order:] for b in both]
-        else:
-            added = [multiply(left_parts(t), q) for t, q in zip(totals, rights)]
-        totals = [jnp.where(sweep < c, t + a, t) for t, a, c in zip(totals, added, counts)]
-    return [t * (1.0 / e) for t, e in zip(totals, energies)]
+    square = multiply(left_parts(ratio), right_parts(ratio))
+    total = identity + ratio
+    right = right_parts(square)
+    both = multiply(jnp.concatenate([left_parts(total), left_parts(square)], axis=0), right)
+    short = total + both[:order]
+    square = both[order:]
+    right = right_parts(square)
+    both = multiply(jnp.concatenate([left_parts(short), left_parts(square)], axis=0), right)
+    total = short + both[:order]
+    square = both[order:]
+    total = total + multiply(left_parts(total), right_parts(square))
+    return jnp.where(count > 2, total, short) * (1.0 / energy)
 
 
 def kernel(
     ranks, moments, points, order, held,
     energy_hbm, count_hbm, strength_hbm, offset_hbm, sigma_hbm, ham_hbm, coupling_hbm,
-    out_ref,
+    out_ref, sigma_ref,
     green, gathered, mixed_out, wide, across, across_t,
-    sigma_ref, ham_ref, coupling_ref, energy_ref, count_ref, strength_ref, offset_ref,
+    ham_ref, coupling_ref, energy_ref, count_ref, strength_ref, offset_ref,
     ready, read_sigma, read_other, send_first, recv_first, send_second, recv_second,
 ):
     devices = ranks * moments
@@ -166,15 +163,17 @@
         return {"energy": other // moments, "mom": lax.rem(other, moments)}
 
     sources = [
-        (ham_hbm, ham_ref), (energy_hbm, energy_ref), (count_hbm, count_ref),
-        (coupling_hbm, coupling_ref), (strength_hbm, strength_ref), (offset_hbm, offset_ref),
+        (coupling_hbm, coupling_ref), (ham_hbm.at[0], ham_ref.at[0]), (ham_hbm.at[1], ham_ref.at[1]),
+        (energy_hbm, energy_ref), (count_hbm, count_ref), (strength_hbm, strength_ref), (offset_hbm, offset_ref),
     ]
     reads = [pltpu.make_async_copy(a, b, read_other.at[n]) for n, (a, b) in enumerate(sources)]
-    sigma_reads = [
-        pltpu.make_async_copy(sigma_hbm.at[point], sigma_ref.at[point], read_sigma.at[point])
-        for point in range(points)
-    ]
-    for read in [reads[0], sigma_reads[0]] + reads[1:4]:
+
+    def sigma_read(point, slab):
+        return pltpu.make_async_copy(
+            sigma_hbm.at[point, slab], sigma_ref.at[point, slab], read_sigma.at[point, slab]
+        )
+
+    for read in [reads[0], reads[1], sigma_read(0, 0), reads[3], reads[4], reads[2], sigma_read(0, 1)]:
         read.start()
     barrier = pltpu.get_barrier_semaphore()
 
@@ -184,21 +183,37 @@
         return carried
 
     lax.fori_loop(0, side, greet, 0)
-    for read in sigma_reads[1:] + reads[4:]:
+    for read in reads[5:]:
         read.start()
+
+    def read_point(point, carried):
+        sigma_read(point, 0).start()
+        sigma_read(point, 1).start()
+        return carried
+
+    lax.fori_loop(1, points, read_point, 0)
 
     row_index = lax.broadcasted_iota(jnp.int32, (order, order), 0)
     identity = (row_index == lax.broadcasted_iota(jnp.int32, (order, order), 1)).astype(jnp.float32)
 
     def tile_of(other, piece):
         return (held - 1 - piece) * devices + other
+
+    quarter = ranks // 4
+    blocks = quarter // 2
+    my_block = lax.rem(lax.div(my_rank, 2), blocks)
+    my_core = lax.rem(my_rank, 2)
 
     def send_over(send):
         def over(index, carried):
             turn = lax.div(index, group)
-            half = turn * (1 - my_side) + (1 - turn) * my_side
-            half = 1 - half
-            send(far_side + half * group + lax.rem(spot + index, group))
+            layer = turn * my_side + (1 - turn) * (1 - my_side)
+            step = group - 1 - lax.rem(index, group)
+            block = lax.rem(my_block + lax.div(step, 2 * moments), blocks)
+            moment = lax.rem(my_moment + lax.rem(lax.div(step, 2), moments), moments)
+            core = lax.rem(my_core + lax.rem(step, 2), 2)
+            rank = (1 - my_side) * (ranks // 2) + layer * quarter + block * 2 + core
+            send(rank * moments + moment)
             return carried
 
         lax.fori_loop(0, side, over, 0)
@@ -210,49 +225,48 @@
 
         lax.fori_loop(1, side, within, 0)
 
-    def first_of(point, piece, cut):
-        semaphore = recv_first.at[piece if piece < early else early + (piece - early) * cuts + cut]
-        chosen = slice(None) if piece < early else pl.ds(cut * width, width)
-        if piece < early:
+    def first_of(piece, semaphore, point=None, cut=None):
+        if cut is None:
             landing = gathered.at[my_moment, piece, my_rank * points + point]
             source_of = lambda other: green.at[point, tile_of(other, piece)]
         else:
-            landing = gathered.at[my_moment, piece, pl.ds(my_rank * points, points), :, chosen]
-            source_of = lambda other: green.at[:, tile_of(other, piece), :, chosen]
+            later, chosen = pl.ds(1, points - 1), pl.ds(cut * width, width)
+            landing = gathered.at[my_moment, piece, pl.ds(my_rank * points + 1, points - 1), :, chosen]
+            source_of = lambda other: green.at[later, tile_of(other, piece), :, chosen]
 
         def send(other):
             pltpu.make_async_remote_copy(
                 src_ref=source_of(other), dst_ref=landing,
-                send_sem=send_first, recv_sem=semaphore,
+                send_sem=send_first, recv_sem=recv_first.at[semaphore],
                 device_id=place_of(other), device_id_type=MESH_ID,
             ).start()
 
         def keep():
-            pltpu.make_async_copy(source_of(me), landing, semaphore).start()
+            pltpu.make_async_copy(source_of(me), landing, recv_first.at[semaphore]).start()
 
         return send, keep
 
-    for read in reads[:3]:
-        read.wait()
+    reads[0].wait()
+    across[...] = right_parts(coupling_ref[...])
+    across_t[...] = left_parts(coupling_ref[...].T)
+    reads[3].wait()
+    reads[4].wait()
+    reads[1].wait()
+    reads[2].wait()
     tiles = order // SUBLANES
 
     def solve(point, carried):
-        pltpu.make_async_copy(sigma_hbm.at[point], sigma_ref.at[point], read_sigma.at[point]).wait()
+        sigma_read(point, 0).wait()
         energy = energy_ref[my_rank * points + point]
         count = count_ref[my_rank * points + point]
         ratio = (ham_ref[0] + sigma_ref[point, 0]) * (1.0 / energy)
-        left_inverse = series([ratio], [energy], [count], identity)[0]
-
-        @pl.when(point == 0)
-        def _():
-            reads[3].wait()
-            across[...] = right_parts(coupling_ref[...])
-            across_t[...] = left_parts(coupling_ref[...].T)
+        left_inverse = series(ratio, energy, count, identity)
 
         coupled = multiply(left_parts(left_inverse), across[...])
         fold = multiply(across_t[...], right_parts(coupled))
+        sigma_read(point, 1).wait()
         ratio = (ham_ref[1] + sigma_ref[point, 1] + fold) * (1.0 / energy)
-        right_green = series([ratio], [energy], [count], identity)[0]
+        right_green = series(ratio, energy, count, identity)
         green[point, tiles:] = right_green.reshape(tiles, SUBLANES, order)
 
         @pl.when(point == 0)
@@ -262,7 +276,7 @@
             pl.semaphore_signal(ready, inc=1, device_id=place_of(mirror), device_id_type=MESH_ID)
 
         for piece in range(early):
-            send_over(first_of(point, piece, 0)[0])
+            send_over(first_of(piece, piece, point=point)[0])
         back = multiply(across_t[...], right_parts(left_inverse))
         inner = multiply(left_parts(coupled), right_parts(right_green))
         left_green = left_inverse + multiply(left_parts(inner), right_parts(back))
@@ -273,21 +287,30 @@
             pl.semaphore_wait(ready, 1)
 
         for piece in range(early):
-            send, keep = first_of(point, piece, 0)
+            send, keep = first_of(piece, piece, point=point)
             keep()
             send_within(send)
+
+        @pl.when(point == 0)
+        def _():
+            for piece in range(early, held):
+                send, keep = first_of(piece, piece, point=0)
+                keep()
+                send_over(send)
+                send_within(send)
+
         return carried
 
     lax.fori_loop(0, points, solve, 0)
 
     for piece in range(early, held):
         for cut in range(cuts):
-            send, keep = first_of(0, piece, cut)
+            send, keep = first_of(piece, held + (piece - early) * cuts + cut, cut=cut)
             keep()
             send_over(send)
             send_within(send)
 
-    for read in reads[4:]:
+    for read in reads[5:]:
         read.wait()
     span = total * SUBLANES
     column = lax.broadcasted_iota(jnp.int32, (SUBLANES, span), 1)
@@ -317,13 +340,25 @@
         weights.append(weight)
 
     wide_parts = left_parts(wide[...])
-    arrivals = [(piece, 0, slice(None)) for piece in range(early)] + [
-        (piece, cut, slice(cut * width, (cut + 1) * width))
-        for piece in range(early, held) for cut in range(cuts)
+    arrivals = [(piece, None) for piece in range(early)] + [
+        (piece, cut) for piece in range(early, held) for cut in range(cuts)
     ]
-    for number, (piece, cut, chosen) in enumerate(arrivals):
-        arrived = gathered.at[:, piece, :, :, chosen]
-        pltpu.make_async_copy(arrived, arrived, recv_first.at[number]).wait()
+
+    def settle(landed, semaphore):
+        pltpu.make_async_copy(landed, landed, recv_first.at[semaphore]).wait()
+
+    for piece, cut in arrivals:
+        if cut is None:
+            chosen = slice(None)
+            settle(gathered.at[:, piece], piece)
+        else:
+            chosen = slice(cut * width, (cut + 1) * width)
+            if cut == 0:
+                settle(gathered.at[:, piece, pl.ds(0, ranks)], piece)
+            settle(
+                gathered.at[:, piece, pl.ds(0, total - ranks), :, chosen],
+                held + (piece - early) * cuts + cut,
+            )
         for moment in range(moments):
             scattered = weights[0] * gathered[moment, piece, :, :, chosen]
             for step in range(1, moments):
@@ -344,8 +379,8 @@
                 device_id_type=MESH_ID,
             ).start()
 
+        send_over(give_back)
         send_within(give_back)
-        send_over(give_back)
         pltpu.make_async_copy(
             mixed_out.at[my_moment, piece, pl.ds(my_rank * points, points), :, chosen],
             out_ref.at[:, tile_of(me, piece), :, chosen],
@@ -369,11 +404,14 @@
     cuts = 2 if order % 256 == 0 else 1
     hbm = pl.BlockSpec(memory_space=pltpu.HBM)
     operands = (energies, counts, strengths, offsets, sigma_in[:, 0], hamiltonian[0], coupling[0])
-    sigma_new = pl.pallas_call(
+    sigma_new, sigma_held = pl.pallas_call(
         functools.partial(kernel, ranks, moments, points, order, held),
-        out_shape=jax.ShapeDtypeStruct((points, tiles, SUBLANES, order), jnp.float32),
+        out_shape=[
+            jax.ShapeDtypeStruct((points, tiles, SUBLANES, order), jnp.float32),
+            jax.ShapeDtypeStruct((points, 2, order, order), jnp.float32),
+        ],
         in_specs=[hbm] * 7,
-        out_specs=pl.BlockSpec(memory_space=pltpu.VMEM),
+        out_specs=[pl.BlockSpec(memory_space=pltpu.VMEM)] * 2,
         scratch_shapes=[
             pltpu.VMEM((points, tiles, SUBLANES, order), jnp.float32),
             pltpu.VMEM((moments, held, total, SUBLANES, order), jnp.float32),
@@ -381,7 +419,6 @@
             pltpu.VMEM((span, span), jnp.float32),
             pltpu.VMEM((3 * order, order), jnp.bfloat16),
             pltpu.VMEM((order, 3 * order), jnp.bfloat16),
-            pltpu.VMEM((points, 2, order, order), jnp.float32),
             pltpu.VMEM((2, order, order), jnp.float32),
             pltpu.VMEM((order, order), jnp.float32),
             pltpu.SMEM(energies.shape, jnp.float32),
@@ -389,10 +426,10 @@
             pltpu.SMEM(strengths.shape, jnp.float32),
             pltpu.SMEM(offsets.shape, jnp.int32),
             pltpu.SemaphoreType.REGULAR,
-            pltpu.SemaphoreType.DMA((points,)),
-            pltpu.SemaphoreType.DMA((6,)),
+            pltpu.SemaphoreType.DMA((points, 2)),
+            pltpu.SemaphoreType.DMA((7,)),
             pltpu.SemaphoreType.DMA,
-            pltpu.SemaphoreType.DMA((held // 2 * (1 + cuts),)),
+            pltpu.SemaphoreType.DMA((held + held // 2 * cuts,)),
             pltpu.SemaphoreType.DMA,
             pltpu.SemaphoreType.DMA,
         ],
@@ -401,13 +438,14 @@
         ),
         name="green_and_scatter",
     )(*[pltpu.with_memory_space_constraint(value, pltpu.HBM) for value in operands])
-    return (1.0 - MIX_RATE) * sigma_in + sigma_new.reshape(sigma_in.shape)
+    result = (1.0 - MIX_RATE) * sigma_held.reshape(sigma_in.shape) + sigma_new.reshape(sigma_in.shape)
+    return result
 
 
 def body(sigma_in, hamiltonian, coupling, energies, counts, strengths, offsets):
     devices = lax.axis_size("energy") * lax.axis_size("mom")
     tiles = 2 * sigma_in.shape[3] // SUBLANES
-    fits = tiles % (2 * devices) == 0 and lax.axis_size("energy") % 4 == 0
+    fits = tiles % (2 * devices) == 0 and lax.axis_size("energy") % 8 == 0 and sigma_in.shape[0] > 1
     chosen = fused_body if fits else plain_body
     return chosen(sigma_in, hamiltonian, coupling, energies, counts, strengths, offsets)
 

time: 101 us -> 100 us (0.990)
  no operation moved by 1% of the time
where the time goes in v2:
time: 100 us
  Pallas kernels  98.4 us (98%)
  other arithmetic  1.59 us (2%)
    pallas_call x1, Pallas kernels, fused_body(): pl.pallas_call(functools.partial(kernel, ranks, moments, points, order, h...  98.4 us

profile of v2, /device:TPU:8, one launch (start us, length us, event | category | flops | bytes accessed | tf_op | source)
XLA Modules:
  0.0 100.0 jit_solution(7658320143672665217)
XLA Ops:
  0.0 98.4 %green_and_scatter.1 = (f32[4,64,8,256]{3,2,1,0:T(8,128)S(1)}, f32[4,2,256,256]{3,2,1,0:T(8,128)S(1)}) custom-call(f32[64]{0:T(128)} %energy_hbm.1, s32[64]{0:T(128)} %count_hbm.1, f32[16]{0:T(128)} %strength_hbm.1, s32[16]{0:T(128)} %offset_hbm.1, f32[4,2,256,256]{3,2,1,0:T(8,128)} %bitcast.13, f32[2,256,256]{2,1,0:T(8,128)} %bitcast.14, f32[256,256]{1,0:T(8,128)} %bitcast.15), custom_call_target="tpu_custom_call" | custom-call | tf_op jit(solution)/shard_map/green_and_scatter/pallas_call | solution.py:407
  98.4 1.6 %fusion = f32[4,1,2,256,256]{4,3,2,1,0:T(8,128)} fusion(f32[4,2,256,256]{3,2,1,0:T(8,128)S(1)} %get-tuple-element.7, f32[4,2,256,256]{3,2,1,0:T(8,128)S(1)} %bitcast.12), kind=kLoop, calls=%fused_computation.1 | loop fusion | flops 1048576 | bytes 6291456 | tf_op jit(solution)/shard_map/add | solution.py:441

commit v3 on v2

--- a/solution.py
+++ b/solution.py
@@ -106,34 +106,44 @@
     return high, (value - high.astype(jnp.float32)).astype(jnp.bfloat16)
 
 
-def left_parts(value):
-    high, low = split(value)
-    return jnp.concatenate([high, low, high], axis=1)
-
-
-def right_parts(value):
-    high, low = split(value)
-    return jnp.concatenate([high, high, low], axis=0)
+left_parts = right_parts = split
 
 
 def multiply(left_side, right_side):
-    return jnp.dot(left_side, right_side, preferred_element_type=jnp.float32)
+    (high, low), (near, far) = left_side, right_side
+    rows = high.shape[0] // 2
+    both = [
+        jnp.dot(jnp.concatenate([high[n * rows:(n + 1) * rows], low[n * rows:(n + 1) * rows]], axis=0), near, preferred_element_type=jnp.float32)
+        for n in range(2)
+    ]
+    last = [jnp.dot(high[n * rows:(n + 1) * rows], far, preferred_element_type=jnp.float32) for n in range(2)]
+    return jnp.concatenate([b[:rows] + b[rows:] + l for b, l in zip(both, last)], axis=0)
 
 
 def series(ratio, energy, count, identity):
-    order = identity.shape[0]
     square = multiply(left_parts(ratio), right_parts(ratio))
     total = identity + ratio
     right = right_parts(square)
-    both = multiply(jnp.concatenate([left_parts(total), left_parts(square)], axis=0), right)
-    short = total + both[:order]
-    square = both[order:]
+    fourth = multiply(left_parts(square), right)
+    short = total + multiply(left_parts(total), right)
+    right = right_parts(fourth)
+    eighth = multiply(left_parts(fourth), right)
+    total = short + multiply(left_parts(short), right)
+    total = total + multiply(left_parts(total), right_parts(eighth))
+    return jnp.where(count > 2, total, short) * (1.0 / energy)
+
+
+def powers(ratio, count, identity):
+    square = multiply(left_parts(ratio), right_parts(ratio))
+    total = identity + ratio
     right = right_parts(square)
-    both = multiply(jnp.concatenate([left_parts(short), left_parts(square)], axis=0), right)
-    total = short + both[:order]
-    square = both[order:]
-    total = total + multiply(left_parts(total), right_parts(square))
-    return jnp.where(count > 2, total, short) * (1.0 / energy)
+    fourth = multiply(left_parts(square), right)
+    short = total + multiply(left_parts(total), right)
+    fourth = jnp.where(count > 2, fourth, 0.0)
+    right = right_parts(fourth)
+    eighth = multiply(left_parts(fourth), right)
+    total = short + multiply(left_parts(short), right)
+    return total, eighth
 
 
 def kernel(
@@ -247,8 +257,8 @@
         return send, keep
 
     reads[0].wait()
-    across[...] = right_parts(coupling_ref[...])
-    across_t[...] = left_parts(coupling_ref[...].T)
+    across[0], across[1] = split(coupling_ref[...])
+    across_t[0], across_t[1] = split(coupling_ref[...].T)
     reads[3].wait()
     reads[4].wait()
     reads[1].wait()
@@ -260,10 +270,11 @@
         energy = energy_ref[my_rank * points + point]
         count = count_ref[my_rank * points + point]
         ratio = (ham_ref[0] + sigma_ref[point, 0]) * (1.0 / energy)
-        left_inverse = series(ratio, energy, count, identity)
-
-        coupled = multiply(left_parts(left_inverse), across[...])
-        fold = multiply(across_t[...], right_parts(coupled))
+        total, last = powers(ratio, count, identity)
+        spread = coupling_ref[...] + multiply(left_parts(last), (across[0], across[1]))
+        back = multiply((across_t[0], across_t[1]), right_parts(total))
+
+        fold = multiply(left_parts(back), right_parts(spread)) * (1.0 / energy)
         sigma_read(point, 1).wait()
         ratio = (ham_ref[1] + sigma_ref[point, 1] + fold) * (1.0 / energy)
         right_green = series(ratio, energy, count, identity)
@@ -277,7 +288,10 @@
 
         for piece in range(early):
             send_over(first_of(piece, piece, point=point)[0])
-        back = multiply(across_t[...], right_parts(left_inverse))
+        right = right_parts(last)
+        left_inverse = (total + multiply(left_parts(total), right)) * (1.0 / energy)
+        back = (back + multiply(left_parts(back), right)) * (1.0 / energy)
+        coupled = multiply(left_parts(total), right_parts(spread)) * (1.0 / energy)
         inner = multiply(left_parts(coupled), right_parts(right_green))
         left_green = left_inverse + multiply(left_parts(inner), right_parts(back))
         green[point, :tiles] = left_green.reshape(tiles, SUBLANES, order)
@@ -417,8 +431,8 @@
             pltpu.VMEM((moments, held, total, SUBLANES, order), jnp.float32),
             pltpu.VMEM((moments, held, total, SUBLANES, order), jnp.float32),
             pltpu.VMEM((span, span), jnp.float32),
-            pltpu.VMEM((3 * order, order), jnp.bfloat16),
-            pltpu.VMEM((order, 3 * order), jnp.bfloat16),
+            pltpu.VMEM((2, order, order), jnp.bfloat16),
+            pltpu.VMEM((2, order, order), jnp.bfloat16),
             pltpu.VMEM((2, order, order), jnp.float32),
             pltpu.VMEM((order, order), jnp.float32),
             pltpu.SMEM(energies.shape, jnp.float32),

time: 100 us -> 98.7 us (0.987)
  Pallas kernels: 98.4 us -> 96.9 us
    pallas_call x1, Pallas kernels: 98.4 us -> 96.9 us  [fused_body(): pl.pallas_call(functools.partial(kernel, ranks, moments, points, order, h...]
where the time goes in v3:
time: 98.7 us; the launch traced here: 98.5 us
  Pallas kernels  96.9 us (98%)
  other arithmetic  1.59 us (2%)
    pallas_call x1, Pallas kernels, fused_body(): pl.pallas_call(functools.partial(kernel, ranks, moments, points, order, h...  96.9 us

profile of v3, /device:TPU:8, one launch (start us, length us, event | category | flops | bytes accessed | tf_op | source)
XLA Modules:
  0.0 98.5 jit_solution(1063137598890618666)
XLA Ops:
  0.0 96.9 %green_and_scatter.1 = (f32[4,64,8,256]{3,2,1,0:T(8,128)S(1)}, f32[4,2,256,256]{3,2,1,0:T(8,128)S(1)}) custom-call(f32[64]{0:T(128)} %energy_hbm.1, s32[64]{0:T(128)} %count_hbm.1, f32[16]{0:T(128)} %strength_hbm.1, s32[16]{0:T(128)} %offset_hbm.1, f32[4,2,256,256]{3,2,1,0:T(8,128)} %bitcast.13, f32[2,256,256]{2,1,0:T(8,128)} %bitcast.14, f32[256,256]{1,0:T(8,128)} %bitcast.15), custom_call_target="tpu_custom_call" | custom-call | tf_op jit(solution)/shard_map/green_and_scatter/pallas_call | solution.py:421
  96.9 1.6 %fusion = f32[4,1,2,256,256]{4,3,2,1,0:T(8,128)} fusion(f32[4,2,256,256]{3,2,1,0:T(8,128)S(1)} %get-tuple-element.7, f32[4,2,256,256]{3,2,1,0:T(8,128)S(1)} %bitcast.12), kind=kLoop, calls=%fused_computation.1 | loop fusion | flops 1048576 | bytes 6291456 | tf_op jit(solution)/shard_map/add | solution.py:455

commit v4 on v3

--- a/solution.py
+++ b/solution.py
@@ -133,8 +133,9 @@
     return jnp.where(count > 2, total, short) * (1.0 / energy)
 
 
-def powers(ratio, count, identity):
+def powers(ratio, count, identity, prepare):
     square = multiply(left_parts(ratio), right_parts(ratio))
+    prepare()
     total = identity + ratio
     right = right_parts(square)
     fourth = multiply(left_parts(square), right)
@@ -183,31 +184,9 @@
             sigma_hbm.at[point, slab], sigma_ref.at[point, slab], read_sigma.at[point, slab]
         )
 
-    for read in [reads[0], reads[1], sigma_read(0, 0), reads[3], reads[4], reads[2], sigma_read(0, 1)]:
+    for read in [reads[1], sigma_read(0, 0), reads[3], reads[4]]:
         read.start()
     barrier = pltpu.get_barrier_semaphore()
-
-    def greet(index, carried):
-        other = far_side + lax.rem(spot + index, side)
-        pl.semaphore_signal(barrier, inc=1, device_id=place_of(other), device_id_type=MESH_ID)
-        return carried
-
-    lax.fori_loop(0, side, greet, 0)
-    for read in reads[5:]:
-        read.start()
-
-    def read_point(point, carried):
-        sigma_read(point, 0).start()
-        sigma_read(point, 1).start()
-        return carried
-
-    lax.fori_loop(1, points, read_point, 0)
-
-    row_index = lax.broadcasted_iota(jnp.int32, (order, order), 0)
-    identity = (row_index == lax.broadcasted_iota(jnp.int32, (order, order), 1)).astype(jnp.float32)
-
-    def tile_of(other, piece):
-        return (held - 1 - piece) * devices + other
 
     quarter = ranks // 4
     blocks = quarter // 2
@@ -228,6 +207,19 @@
 
         lax.fori_loop(0, side, over, 0)
 
+    def greet(other):
+        pl.semaphore_signal(barrier, inc=1, device_id=place_of(other), device_id_type=MESH_ID)
+
+    send_over(greet)
+    for read in [reads[0], reads[2], sigma_read(0, 1)]:
+        read.start()
+
+    row_index = lax.broadcasted_iota(jnp.int32, (order, order), 0)
+    identity = (row_index == lax.broadcasted_iota(jnp.int32, (order, order), 1)).astype(jnp.float32)
+
+    def tile_of(other, piece):
+        return (held - 1 - piece) * devices + other
+
     def send_within(send):
         def within(index, carried):
             send(near_side + lax.rem(spot + index, side))
@@ -256,38 +248,63 @@
 
         return send, keep
 
-    reads[0].wait()
-    across[0], across[1] = split(coupling_ref[...])
-    across_t[0], across_t[1] = split(coupling_ref[...].T)
-    reads[3].wait()
-    reads[4].wait()
-    reads[1].wait()
-    reads[2].wait()
+    for read in [reads[3], reads[4], reads[1], sigma_read(0, 0)]:
+        read.wait()
     tiles = order // SUBLANES
 
-    def solve(point, carried):
-        sigma_read(point, 0).wait()
+    def solve(point, first):
+        if not first:
+            sigma_read(point, 0).wait()
+            sigma_read(point, 1).wait()
         energy = energy_ref[my_rank * points + point]
         count = count_ref[my_rank * points + point]
         ratio = (ham_ref[0] + sigma_ref[point, 0]) * (1.0 / energy)
-        total, last = powers(ratio, count, identity)
+
+        def prepare():
+            if first:
+                reads[0].wait()
+                across[0], across[1] = split(coupling_ref[...])
+                across_t[0], across_t[1] = split(coupling_ref[...].T)
+
+        total, last = powers(ratio, count, identity, prepare)
         spread = coupling_ref[...] + multiply(left_parts(last), (across[0], across[1]))
         back = multiply((across_t[0], across_t[1]), right_parts(total))
 
         fold = multiply(left_parts(back), right_parts(spread)) * (1.0 / energy)
-        sigma_read(point, 1).wait()
+        if first:
+            reads[2].wait()
+            sigma_read(0, 1).wait()
         ratio = (ham_ref[1] + sigma_ref[point, 1] + fold) * (1.0 / energy)
         right_green = series(ratio, energy, count, identity)
         green[point, tiles:] = right_green.reshape(tiles, SUBLANES, order)
 
-        @pl.when(point == 0)
-        def _():
+        if first:
             pl.semaphore_wait(barrier, side)
             mirror = lax.rem(me + side, devices)
             pl.semaphore_signal(ready, inc=1, device_id=place_of(mirror), device_id_type=MESH_ID)
 
         for piece in range(early):
             send_over(first_of(piece, piece, point=point)[0])
+        if first:
+            for read in reads[5:]:
+                read.start()
+
+            def read_point(point, carried):
+                sigma_read(point, 0).start()
+                sigma_read(point, 1).start()
+                return carried
+
+            lax.fori_loop(1, points, read_point, 0)
+        else:
+
+            @pl.when(point == 1)
+            def _():
+                pl.semaphore_wait(ready, 1)
+                for piece in range(held):
+                    send, keep = first_of(piece, piece, point=0)
+                    keep()
+                    send_within(send)
+
         right = right_parts(last)
         left_inverse = (total + multiply(left_parts(total), right)) * (1.0 / energy)
         back = (back + multiply(left_parts(back), right)) * (1.0 / energy)
@@ -296,26 +313,21 @@
         left_green = left_inverse + multiply(left_parts(inner), right_parts(back))
         green[point, :tiles] = left_green.reshape(tiles, SUBLANES, order)
 
-        @pl.when(point == 0)
-        def _():
-            pl.semaphore_wait(ready, 1)
-
-        for piece in range(early):
-            send, keep = first_of(piece, piece, point=point)
-            keep()
-            send_within(send)
-
-        @pl.when(point == 0)
-        def _():
+        if first:
             for piece in range(early, held):
-                send, keep = first_of(piece, piece, point=0)
+                send_over(first_of(piece, piece, point=0)[0])
+        else:
+            for piece in range(early):
+                send, keep = first_of(piece, piece, point=point)
                 keep()
-                send_over(send)
                 send_within(send)
 
+    def solve_later(point, carried):
+        solve(point, False)
         return carried
 
-    lax.fori_loop(0, points, solve, 0)
+    solve(0, True)
+    lax.fori_loop(1, points, solve_later, 0)
 
     for piece in range(early, held):
         for cut in range(cuts):
@@ -405,6 +417,19 @@
     sent = green.at[:, pl.ds(0, (devices - 1) * held)]
     pltpu.make_async_copy(sent, sent, send_first).wait()
     pltpu.make_async_copy(sent, sent, send_second).wait()
+
+
+def finish(parts, sigma_ref, new_ref, out_hbm, mixed, done):
+    rows = sigma_ref.shape[0] // parts
+    copies = []
+    for part in range(parts):
+        chosen = pl.ds(part * rows, rows)
+        mixed[chosen] = (1.0 - MIX_RATE) * sigma_ref[chosen] + new_ref[chosen]
+        copy = pltpu.make_async_copy(mixed.at[chosen], out_hbm.at[chosen], done.at[part])
+        copy.start()
+        copies.append(copy)
+    for copy in copies:
+        copy.wait()
 
 
 def fused_body(sigma_in, hamiltonian, coupling, energies, counts, strengths, offsets):
@@ -452,8 +477,19 @@
         ),
         name="green_and_scatter",
     )(*[pltpu.with_memory_space_constraint(value, pltpu.HBM) for value in operands])
-    result = (1.0 - MIX_RATE) * sigma_held.reshape(sigma_in.shape) + sigma_new.reshape(sigma_in.shape)
-    return result
+    cells = (points * tiles, SUBLANES, order)
+    vmem = pl.BlockSpec(memory_space=pltpu.VMEM)
+    parts = 4
+    result = pl.pallas_call(
+        functools.partial(finish, parts),
+        out_shape=jax.ShapeDtypeStruct(cells, jnp.float32),
+        in_specs=[vmem] * 2,
+        out_specs=pl.BlockSpec(memory_space=pltpu.HBM),
+        scratch_shapes=[pltpu.VMEM(cells, jnp.float32), pltpu.SemaphoreType.DMA((parts,))],
+        compiler_params=pltpu.CompilerParams(vmem_limit_bytes=8 * 1024 * 1024),
+        name="mix",
+    )(sigma_held.reshape(cells), sigma_new.reshape(cells))
+    return result.reshape(sigma_in.shape)
 
 
 def body(sigma_in, hamiltonian, coupling, energies, counts, strengths, offsets):

time: 98.7 us -> 98.4 us (level)
  other arithmetic: 1.59 us -> 0 us
  Pallas kernels: 96.9 us -> 98.2 us
    add x1 -> x0, other arithmetic: 1.59 us -> none  [fused_body(): (1.0 - MIX_RATE) * sigma_held.reshape(sigma_in.shape)]
    pallas_call x0 -> x1, Pallas kernels: none -> 1.41 us  [fused_body(): pl.pallas_call(functools.partial(finish, parts), out_shape=jax.ShapeDtype...]
where the time goes in v4:
time: 98.4 us; the launch traced here: 98.2 us
  Pallas kernels  98.2 us (100%)
    pallas_call x1, Pallas kernels, fused_body(): pl.pallas_call(functools.partial(kernel, ranks, moments, points, order, h...  96.8 us

profile of v4, /device:TPU:8, one launch (start us, length us, event | category | flops | bytes accessed | tf_op | source)
XLA Modules:
  0.0 98.2 jit_solution(8994562025239941677)
XLA Ops:
  0.0 96.8 %green_and_scatter.1 = (f32[4,64,8,256]{3,2,1,0:T(8,128)S(1)}, f32[4,2,256,256]{3,2,1,0:T(8,128)S(1)}) custom-call(f32[64]{0:T(128)} %energy_hbm.1, s32[64]{0:T(128)} %count_hbm.1, f32[16]{0:T(128)} %strength_hbm.1, s32[16]{0:T(128)} %offset_hbm.1, f32[4,2,256,256]{3,2,1,0:T(8,128)} %bitcast.10, f32[2,256,256]{2,1,0:T(8,128)} %bitcast.11, f32[256,256]{1,0:T(8,128)} %bitcast.12), custom_call_target="tpu_custom_call" | custom-call | tf_op jit(solution)/shard_map/green_and_scatter/pallas_call | solution.py:446
  96.8 1.4 %mix.1 = f32[256,8,256]{2,1,0:T(8,128)} custom-call(f32[256,8,256]{2,1,0:T(8,128)S(1)} %bitcast.9, f32[256,8,256]{2,1,0:T(8,128)S(1)} %bitcast.8), custom_call_target="tpu_custom_call" | custom-call | tf_op jit(solution)/shard_map/mix/pallas_call | solution.py:483
